TPU v7x, 32 devices: a whole 2x2x4 slice. The times are simulated.
32 devices in a mesh: node: 8 (over z, core), dev: 4 (over y, x).
Axes of the slice: x: 2, y: 2, z: 4, core: 2. Of those that a mesh axis runs over, the one named last changes fastest.
Arguments:
- blocks: bfloat16 [8, 4, 16, 7, 16, 256], P('node', 'dev'), may hold values from -6 to 6
- levels: int32 [8, 4, 16], P('node', 'dev'), may hold values from 0 to 3
- destinations: int32 [8, 4, 16], P('node', 'dev'), may hold values from 0 to 3, as said below
- speeds: float32 [7], replicated, may hold values from -1 to 1
- thresholds: float32 [7], replicated, may hold values from 0.1 to 1
Outputs:
- updated: bfloat16 [8, 4, 32, 7, 16, 256], P('node', 'dev')
- new_levels: int32 [8, 4, 32], P('node', 'dev')
Inputs may be any that keep to these rules, and one draw needn't show every extreme that they name: `destinations`: at most 8 blocks of one device go to one device, and at most 32 blocks arrive at one device; in every group both bounds are reached.
All inputs are finite; a program needn't handle non-finite values.
Results may differ from a plain program's by a relative error of at most 0.001.
Values may be sent and summed in bfloat16 or wider, within the bound.
A program may use at most 64 MiB of HBM per device.

v0:
```python
import jax
import jax.numpy as jnp
from jax import lax
from jax.sharding import PartitionSpec as P

QUANT = 7
EDGE = 16
SLOTS = 16
NEW_CAP = 32


COURANT = 0.4
WENO_EPS = 1e-06


def extended_2(block, sides, width):
    for axis, dim in sides:
        count = lax.axis_size(axis)
        forward = [(i, i + 1) for i in range(count - 1)]
        backward = [(target, source) for source, target in forward]
        low = lax.ppermute(
            lax.slice_in_dim(block, block.shape[dim] - width, None, axis=dim), axis, forward
        )
        high = lax.ppermute(lax.slice_in_dim(block, 0, width, axis=dim), axis, backward)
        block = jnp.concatenate([low, block, high], axis=dim)
    return block


def square(value):
    return value * value


def weno_face(first, second, third, fourth, fifth):
    guess_zero = (2.0 * first - 7.0 * second + 11.0 * third) / 6.0
    guess_one = (-second + 5.0 * third + 2.0 * fourth) / 6.0
    guess_two = (2.0 * third + 5.0 * fourth - fifth) / 6.0
    smooth_zero = 13.0 / 12.0 * square(first - 2.0 * second + third) + 0.25 * square(
        first - 4.0 * second + 3.0 * third
    )
    smooth_one = 13.0 / 12.0 * square(second - 2.0 * third + fourth) + 0.25 * square(
        second - fourth
    )
    smooth_two = 13.0 / 12.0 * square(third - 2.0 * fourth + fifth) + 0.25 * square(
        3.0 * third - 4.0 * fourth + fifth
    )
    weight_zero = 0.1 / square(WENO_EPS + smooth_zero)
    weight_one = 0.6 / square(WENO_EPS + smooth_one)
    weight_two = 0.3 / square(WENO_EPS + smooth_two)
    total = weight_zero + weight_one + weight_two
    return (weight_zero * guess_zero + weight_one * guess_one + weight_two * guess_two) / total


def shape_ghosts(near_layers, near_tag, own_tag):
    same_level = near_layers[:, :, 0:3]
    finer_level = 0.5 * (near_layers[:, :, 0:6:2] + near_layers[:, :, 1:6:2])
    coarser = jnp.concatenate(
        [near_layers[:, :, 0:1], near_layers[:, :, 0:1], near_layers[:, :, 1:2]], axis=2
    )
    offset = jnp.clip(near_tag - own_tag, -1, 1)[:, None, None, None]
    ghost_cells = jnp.where(offset > 0, finer_level, jnp.where(offset < 0, coarser, same_level))
    return lax.optimization_barrier(ghost_cells.astype(jnp.bfloat16))


def advance_quantity(extended, occupied, velocity, threshold):
    cells = extended.shape[1] - 6
    stencil = [extended[:, k : k + cells + 1] for k in range(6)]
    left_state = weno_face(stencil[0], stencil[1], stencil[2], stencil[3], stencil[4])
    right_state = weno_face(stencil[5], stencil[4], stencil[3], stencil[2], stencil[1])
    fluxes = jnp.maximum(velocity, 0.0) * left_state + jnp.minimum(velocity, 0.0) * right_state
    advanced = extended[:, 3 : 3 + cells] - COURANT * (fluxes[:, 1:] - fluxes[:, :-1])
    even_cells = advanced[:, 0::2]
    odd_cells = advanced[:, 1::2]
    predicted = jnp.concatenate(
        [0.5 * (even_cells[:, :-1] + even_cells[:, 1:]), even_cells[:, -1:]], axis=1
    )
    detail = odd_cells - predicted
    kept_cells = predicted + detail - jnp.clip(detail, -threshold, threshold)
    result = jnp.stack([even_cells, kept_cells], axis=2).reshape(advanced.shape)
    return jnp.where(occupied[:, None, None], result, 0.0).astype(jnp.bfloat16)


def body(blocks, levels, destinations, speeds, thresholds):
    owners = lax.axis_size("dev")
    pair_slots = max(1, (2 * SLOTS + owners - 1) // owners)
    send_rows = owners * pair_slots
    plane_cells = EDGE * EDGE
    targets = destinations[0, 0]
    matches = (targets[:, None] == jnp.arange(owners, dtype=jnp.int32)[None, :]).astype(jnp.int32)
    within = jnp.sum((jnp.cumsum(matches, axis=0) - matches) * matches, axis=1)
    buffer_row = targets * pair_slots + within
    placing = (buffer_row[None, :] == jnp.arange(send_rows, dtype=jnp.int32)[:, None]).astype(
        jnp.bfloat16
    )
    payload = blocks.reshape(SLOTS, QUANT * EDGE * plane_cells)
    outgoing = jnp.dot(placing, payload, preferred_element_type=jnp.float32).astype(jnp.bfloat16)
    level_tags = (levels[0, 0] + 1).astype(jnp.bfloat16)[:, None]
    outgoing_tags = jnp.dot(placing, level_tags, preferred_element_type=jnp.float32).astype(
        jnp.bfloat16
    )[:, 0]
    incoming, incoming_tags = (
        lax.all_to_all(outgoing, "dev", split_axis=0, concat_axis=0, tiled=True),
        lax.all_to_all(outgoing_tags, "dev", split_axis=0, concat_axis=0, tiled=True),
    )
    present = (incoming_tags > 0).astype(jnp.int32)
    packed_rank = jnp.cumsum(present) - present
    packing = (
        (packed_rank[None, :] == jnp.arange(NEW_CAP, dtype=jnp.int32)[:, None])
        & (present[None, :] > 0)
    ).astype(jnp.bfloat16)
    arranged = jnp.dot(packing, incoming, preferred_element_type=jnp.float32).astype(jnp.bfloat16)
    arranged = arranged.reshape(NEW_CAP, QUANT, EDGE, plane_cells)
    block_tag = jnp.dot(packing, incoming_tags[:, None], preferred_element_type=jnp.float32)[
        :, 0
    ].astype(jnp.int32)
    near_tags = extended_2(block_tag[:, None], (("node", 1),), 1)
    top_layers = arranged[:, :, EDGE - 6 :].astype(jnp.float32)[:, :, ::-1]
    bottom_layers = arranged[:, :, :6].astype(jnp.float32)
    for_above = shape_ghosts(top_layers, block_tag, near_tags[:, 2])[:, :, ::-1]
    for_below = shape_ghosts(bottom_layers, block_tag, near_tags[:, 0])
    received = extended_2(jnp.concatenate([for_below, for_above], axis=2), (("node", 2),), 3)
    ghost_low = received[:, :, 0:3]
    ghost_high = received[:, :, 9:12]
    extended = jnp.concatenate([ghost_low, arranged, ghost_high], axis=2).astype(jnp.float32)
    extended = jnp.moveaxis(extended, 1, 0)
    occupied = block_tag > 0
    result = lax.map(
        lambda entry: advance_quantity(entry[0], occupied, entry[1], entry[2]),
        (extended, speeds, thresholds),
    )
    updated = jnp.moveaxis(result, 0, 1).reshape(1, 1, NEW_CAP, QUANT, EDGE, plane_cells)
    new_levels = (block_tag - 1).reshape(1, 1, NEW_CAP)
    return (updated, new_levels)


def solution(mesh):
    return jax.shard_map(
        body,
        mesh=mesh,
        in_specs=(
            P("node", "dev", None, None, None, None),
            P("node", "dev", None),
            P("node", "dev", None),
            P(),
            P(),
        ),
        out_specs=(P("node", "dev", None, None, None, None), P("node", "dev", None)),
        check_vma=False,
    )
```

profile of v0, /device:TPU:1, one launch (start us, length us, event | category | flops | bytes accessed | tf_op | source)
XLA Modules:
  0.0 121.0 jit_solution(16075377132843280999)
XLA Ops:
  0.6 0.7 fusion.42
  1.4 0.8 select_reduce_fusion
  2.9 0.8 fusion.29
  4.3 4.3 %all-to-all-start = ((bf16[4,8,1]{1,2,0:T(2,128)(2,1)}), bf16[4,8,1]{1,2,0:T(2,128)(2,1)S(1)}, u32[]{:S(2)}, u32[]{:S(2)}) async-start(bf16[4,8,1]{1,2,0:T(2,128)(2,1)} %all_to_all.22), calls=%async_computation | async-start | bytes 4096 | tf_op jit(solution)/shard_map/all_to_all | solution.py:102
  8.6 1.6 %reshape.147 = bf16[16,28672]{1,0:T(8,128)(2,1)S(1)} reshape(bf16[1,1,16,7,16,256]{5,4,3,2,1,0:T(8,128)(2,1)} %param.7) | data formatting | bytes 1835008 | tf_op jit(solution)/shard_map/reshape | solution.py:94
  10.2 1.9 %fusion.27 = bf16[4,8,28672]{2,1,0:T(8,128)(2,1)} fusion(bf16[16,28672]{1,0:T(8,128)(2,1)S(1)} %reshape.147, s32[16]{0:T(128)S(1)} %multiply_add_fusion.3), kind=kOutput, calls=%fused_computation.43 | convolution fusion | flops 30278144 | bytes 2752576 | tf_op jit(solution)/shard_map/dot_general | solution.py:95
  12.1 3.6 %all-to-all-start.1 = ((bf16[4,8,28672]{2,1,0:T(8,128)(2,1)}), bf16[4,8,28672]{2,1,0:T(8,128)(2,1)S(1)}, u32[]{:S(2)}, u32[]{:S(2)}) async-start(bf16[4,8,28672]{2,1,0:T(8,128)(2,1)} %fusion.27), calls=%async_computation.1 | async-start | bytes 3670016 | tf_op jit(solution)/shard_map/all_to_all | solution.py:101
  16.3 3.9 %collective-permute-start = (s32[32,1]{0,1:T(1,128)S(1)}, s32[32,1]{0,1:T(1,128)S(1)}, u32[]{:S(2)}, u32[]{:S(2)}) collective-permute-start(s32[32,1]{0,1:T(1,128)S(1)} %bitcast.80), channel_id=1, source_target_pairs={{4,0},{8,4},{12,8},{16,12},{20,16},{24,20},{28,24},{5,1},{9,5},{13... | collective-permute-start | bytes 392 | tf_op jit(solution)/shard_map/ppermute | solution.py:24
  20.2 3.1 %collective-permute-start.2 = (s32[32,1]{0,1:T(1,128)S(1)}, s32[32,1]{0,1:T(1,128)S(1)}, u32[]{:S(2)}, u32[]{:S(2)}) collective-permute-start(s32[32,1]{0,1:T(1,128)S(1)} %bitcast.81), channel_id=1, source_target_pairs={{0,4},{4,8},{8,12},{12,16},{16,20},{20,24},{24,28},{1,5},{5,9},{9,... | collective-permute-start | bytes 392 | tf_op jit(solution)/shard_map/ppermute | solution.py:21
  24.6 12.6 %all-to-all-done.1 = bf16[4,8,28672]{2,1,0:T(8,128)(2,1)S(1)} async-done(((bf16[4,8,28672]{2,1,0:T(8,128)(2,1)}), bf16[4,8,28672]{2,1,0:T(8,128)(2,1)S(1)}, u32[]{:S(2)}, u32[]{:S(2)}) %all-to-all-start.1) | async-done | bytes 1835040 | tf_op jit(solution)/shard_map/all_to_all | solution.py:101
  38.3 0.7 copy.42
  39.4 0.7 slice.125
  41.2 0.7 rev.4
  41.9 4.5 %collective-permute-start.1 = (bf16[32,7,3,256]{3,0,2,1:T(8,128)(2,1)}, bf16[32,7,3,256]{3,0,2,1:T(8,128)(2,1)}, u32[]{:S(2)}, u32[]{:S(2)}) collective-permute-start(bf16[32,7,3,256]{3,0,2,1:T(8,128)(2,1)} %rev.4), channel_id=1, source_target_pairs={{0,4},{4,8},{8,12},{12,16},{16,20},{20,24},{24,28},{1,5},{5,9},{9,... | collective-permute-start | bytes 1032200 | tf_op jit(solution)/shard_map/ppermute | solution.py:21
  46.4 1.3 %fusion.32 = bf16[32,7,3,256]{3,0,2,1:T(8,128)(2,1)S(1)} fusion(f32[32,7,6,256]{3,0,2,1:T(8,128)S(1)} %get-tuple-element.50, bf16[32,7,2,256]{3,0,2,1:T(8,128)(2,1)} %slice.125, bf16[32,7,1,256]{3,0,2,1:T(8,128)(2,1)} %slice.124, pred[32]{0:T(512)(128)(4,1)} %get-tuple-element.59, pred[32]{0:T(512)(128)(4,1)} %get-tuple-element.60), kind=kLoop, calls=%fused_computation.52 | loop fusion | flops 1376256 | bytes 2752576 | tf_op jit(solution)/shard_map/convert_element_type | solution.py:61
  47.8 1.9 %collective-permute-start.3 = (bf16[32,7,3,256]{3,0,2,1:T(8,128)(2,1)S(1)}, bf16[32,7,3,256]{3,0,2,1:T(8,128)(2,1)S(1)}, u32[]{:S(2)}, u32[]{:S(2)}) collective-permute-start(bf16[32,7,3,256]{3,0,2,1:T(8,128)(2,1)S(1)} %fusion.32), channel_id=1, source_target_pairs={{4,0},{8,4},{12,8},{16,12},{20,16},{24,20},{28,24},{5,1},{9,5},{13... | collective-permute-start | bytes 1032200 | tf_op jit(solution)/shard_map/ppermute | solution.py:24
  49.7 1.1 add_bitcast_fusion
  50.9 5.4 %collective-permute-done.3 = bf16[32,7,3,256]{3,0,2,1:T(8,128)(2,1)S(1)} collective-permute-done((bf16[32,7,3,256]{3,0,2,1:T(8,128)(2,1)S(1)}, bf16[32,7,3,256]{3,0,2,1:T(8,128)(2,1)S(1)}, u32[]{:S(2)}, u32[]{:S(2)}) %collective-permute-start.3) | collective-permute-done | bytes 344096 | tf_op jit(solution)/shard_map/ppermute | solution.py:24
  56.4 3.6 %convert_bitcast_fusion = f32[7,32,22,256]{3,1,2,0:T(8,128)} fusion(bf16[32,7,3,256]{3,0,2,1:T(8,128)(2,1)S(1)} %collective-permute-done.3, bf16[32,7,16,256]{3,0,2,1:T(8,128)(2,1)S(1)} %copy.42, bf16[32,7,3,256]{3,0,2,1:T(8,128)(2,1)} %collective-permute-done.1), kind=kLoop, calls=%fused_computation.44 | loop fusion | flops 3784704 | bytes 7569408 | tf_op jit(solution)/shard_map/transpose | solution.py:124
  60.0 61.0 %while.10 = (s32[]{:T(128)}, bf16[7,32,16,256]{3,2,0,1:T(8,128)(2,1)}, pred[32]{0:T(512)(128)(4,1)S(1)}, f32[7,32,22,256]{3,1,2,0:T(8,128)}, f32[7]{0:T(128)S(1)}, /*index=5*/f32[7]{0:T(128)S(1)}, s32[]{:T(128)}, f32[1]{0:T(128)}) while((s32[]{:T(128)}, bf16[7,32,16,256]{3,2,0,1:T(8,128)(2,1)}, pred[32]{0:T(512)(128)(4,1)S(1)}, ...), condition=%wide.region_4.5_spmd, body=%wide.region_3.4_spmd.sunk | while | flops 18915332 | bytes 11731649 | solution.py:126
  61.9 1.2 dynamic-slice_bitcast_fusion.2
  63.0 2.5 %multiply_add_fusion.5 = f32[32,17,256]{2,0,1:T(8,128)S(1)} fusion(f32[32,22,256]{2,0,1:T(8,128)S(1)} %dynamic-slice_bitcast_fusion.2, f32[]{:T(128)} %bitcast.73, f32[]{:T(128)} %bitcast.74), kind=kLoop, calls=%fused_computation.1.clone.1 | loop fusion | flops 17686528 | bytes 3899400 | tf_op jit(solution)/shard_map/while/body/eval_jaxpr/add | solution.py:69
  67.0 0.7 slice_bitcast_fusion.2
  67.8 0.9 copy_dynamic-update-slice_fusion.2
  70.6 1.2 dynamic-slice_bitcast_fusion.2
  71.8 2.5 %multiply_add_fusion.5 = f32[32,17,256]{2,0,1:T(8,128)S(1)} fusion(f32[32,22,256]{2,0,1:T(8,128)S(1)} %dynamic-slice_bitcast_fusion.2, f32[]{:T(128)} %bitcast.73, f32[]{:T(128)} %bitcast.74), kind=kLoop, calls=%fused_computation.1.clone.1 | loop fusion | flops 17686528 | bytes 3899400 | tf_op jit(solution)/shard_map/while/body/eval_jaxpr/add | solution.py:69
  75.7 0.7 slice_bitcast_fusion.2
  76.6 0.9 copy_dynamic-update-slice_fusion.2
  79.3 1.2 dynamic-slice_bitcast_fusion.2
  80.5 2.5 %multiply_add_fusion.5 = f32[32,17,256]{2,0,1:T(8,128)S(1)} fusion(f32[32,22,256]{2,0,1:T(8,128)S(1)} %dynamic-slice_bitcast_fusion.2, f32[]{:T(128)} %bitcast.73, f32[]{:T(128)} %bitcast.74), kind=kLoop, calls=%fused_computation.1.clone.1 | loop fusion | flops 17686528 | bytes 3899400 | tf_op jit(solution)/shard_map/while/body/eval_jaxpr/add | solution.py:69
  84.4 0.7 slice_bitcast_fusion.2
  85.3 0.9 copy_dynamic-update-slice_fusion.2
  88.0 1.2 dynamic-slice_bitcast_fusion.2
  89.2 2.5 %multiply_add_fusion.5 = f32[32,17,256]{2,0,1:T(8,128)S(1)} fusion(f32[32,22,256]{2,0,1:T(8,128)S(1)} %dynamic-slice_bitcast_fusion.2, f32[]{:T(128)} %bitcast.73, f32[]{:T(128)} %bitcast.74), kind=kLoop, calls=%fused_computation.1.clone.1 | loop fusion | flops 17686528 | bytes 3899400 | tf_op jit(solution)/shard_map/while/body/eval_jaxpr/add | solution.py:69
  93.1 0.7 slice_bitcast_fusion.2
  94.0 0.9 copy_dynamic-update-slice_fusion.2
  96.7 1.2 dynamic-slice_bitcast_fusion.2
  97.9 2.5 %multiply_add_fusion.5 = f32[32,17,256]{2,0,1:T(8,128)S(1)} fusion(f32[32,22,256]{2,0,1:T(8,128)S(1)} %dynamic-slice_bitcast_fusion.2, f32[]{:T(128)} %bitcast.73, f32[]{:T(128)} %bitcast.74), kind=kLoop, calls=%fused_computation.1.clone.1 | loop fusion | flops 17686528 | bytes 3899400 | tf_op jit(solution)/shard_map/while/body/eval_jaxpr/add | solution.py:69
  101.8 0.7 slice_bitcast_fusion.2
  102.7 0.9 copy_dynamic-update-slice_fusion.2
  105.4 1.2 dynamic-slice_bitcast_fusion.2
  106.6 2.5 %multiply_add_fusion.5 = f32[32,17,256]{2,0,1:T(8,128)S(1)} fusion(f32[32,22,256]{2,0,1:T(8,128)S(1)} %dynamic-slice_bitcast_fusion.2, f32[]{:T(128)} %bitcast.73, f32[]{:T(128)} %bitcast.74), kind=kLoop, calls=%fused_computation.1.clone.1 | loop fusion | flops 17686528 | bytes 3899400 | tf_op jit(solution)/shard_map/while/body/eval_jaxpr/add | solution.py:69
  110.5 0.7 slice_bitcast_fusion.2
  111.4 0.9 copy_dynamic-update-slice_fusion.2
  114.1 1.2 dynamic-slice_bitcast_fusion.2
  115.3 2.5 %multiply_add_fusion.5 = f32[32,17,256]{2,0,1:T(8,128)S(1)} fusion(f32[32,22,256]{2,0,1:T(8,128)S(1)} %dynamic-slice_bitcast_fusion.2, f32[]{:T(128)} %bitcast.73, f32[]{:T(128)} %bitcast.74), kind=kLoop, calls=%fused_computation.1.clone.1 | loop fusion | flops 17686528 | bytes 3899400 | tf_op jit(solution)/shard_map/while/body/eval_jaxpr/add | solution.py:69
  119.2 0.7 slice_bitcast_fusion.2
  120.1 0.9 copy_dynamic-update-slice_fusion.2
  (102 shorter events, 16.4 us)
Async XLA Ops:
  4.3 7.8 %all-to-all-start = ((bf16[4,8,1]{1,2,0:T(2,128)(2,1)}), bf16[4,8,1]{1,2,0:T(2,128)(2,1)S(1)}, u32[]{:S(2)}, u32[]{:S(2)}) async-start(bf16[4,8,1]{1,2,0:T(2,128)(2,1)} %all_to_all.22), calls=%async_computation | async-start | bytes 4096 | tf_op jit(solution)/shard_map/all_to_all | solution.py:102
  12.1 25.1 %all-to-all-start.1 = ((bf16[4,8,28672]{2,1,0:T(8,128)(2,1)}), bf16[4,8,28672]{2,1,0:T(8,128)(2,1)S(1)}, u32[]{:S(2)}, u32[]{:S(2)}) async-start(bf16[4,8,28672]{2,1,0:T(8,128)(2,1)} %fusion.27), calls=%async_computation.1 | async-start | bytes 3670016 | tf_op jit(solution)/shard_map/all_to_all | solution.py:101
  16.3 7.7 %copy-start.3 = (s32[32]{0:T(128)}, s32[32]{0:T(128)S(1)}, u32[]{:S(2)}) copy-start(s32[32]{0:T(128)S(1)} %fusion.30) | copy-start | bytes 388
  16.3 7.0 %collective-permute-start = (s32[32,1]{0,1:T(1,128)S(1)}, s32[32,1]{0,1:T(1,128)S(1)}, u32[]{:S(2)}, u32[]{:S(2)}) collective-permute-start(s32[32,1]{0,1:T(1,128)S(1)} %bitcast.80), channel_id=1, source_target_pairs={{4,0},{8,4},{12,8},{16,12},{20,16},{24,20},{28,24},{5,1},{9,5},{13... | collective-permute-start | bytes 392 | tf_op jit(solution)/shard_map/ppermute | solution.py:24
  20.2 3.8 %collective-permute-start.2 = (s32[32,1]{0,1:T(1,128)S(1)}, s32[32,1]{0,1:T(1,128)S(1)}, u32[]{:S(2)}, u32[]{:S(2)}) collective-permute-start(s32[32,1]{0,1:T(1,128)S(1)} %bitcast.81), channel_id=1, source_target_pairs={{0,4},{4,8},{8,12},{12,16},{16,20},{20,24},{24,28},{1,5},{5,9},{9,... | collective-permute-start | bytes 392 | tf_op jit(solution)/shard_map/ppermute | solution.py:21
  39.2 1.6 %copy-start.1 = (pred[32]{0:T(512)(128)(4,1)S(1)}, pred[32]{0:T(512)(128)(4,1)}, u32[]{:S(2)}) copy-start(pred[32]{0:T(512)(128)(4,1)} %get-tuple-element.55) | copy-start | bytes 100
  39.2 1.6 %copy-start.2 = (pred[32]{0:T(512)(128)(4,1)S(1)}, pred[32]{0:T(512)(128)(4,1)}, u32[]{:S(2)}) copy-start(pred[32]{0:T(512)(128)(4,1)} %get-tuple-element.56) | copy-start | bytes 100
  41.9 9.0 %collective-permute-start.1 = (bf16[32,7,3,256]{3,0,2,1:T(8,128)(2,1)}, bf16[32,7,3,256]{3,0,2,1:T(8,128)(2,1)}, u32[]{:S(2)}, u32[]{:S(2)}) collective-permute-start(bf16[32,7,3,256]{3,0,2,1:T(8,128)(2,1)} %rev.4), channel_id=1, source_target_pairs={{0,4},{4,8},{8,12},{12,16},{16,20},{20,24},{24,28},{1,5},{5,9},{9,... | collective-permute-start | bytes 1032200 | tf_op jit(solution)/shard_map/ppermute | solution.py:21
  47.8 8.6 %collective-permute-start.3 = (bf16[32,7,3,256]{3,0,2,1:T(8,128)(2,1)S(1)}, bf16[32,7,3,256]{3,0,2,1:T(8,128)(2,1)S(1)}, u32[]{:S(2)}, u32[]{:S(2)}) collective-permute-start(bf16[32,7,3,256]{3,0,2,1:T(8,128)(2,1)S(1)} %fusion.32), channel_id=1, source_target_pairs={{4,0},{8,4},{12,8},{16,12},{20,16},{24,20},{28,24},{5,1},{9,5},{13... | collective-permute-start | bytes 1032200 | tf_op jit(solution)/shard_map/ppermute | solution.py:24
  50.9 9.1 %copy-start = (pred[32]{0:T(512)(128)(4,1)S(1)}, pred[32]{0:T(512)(128)(4,1)}, u32[]{:S(2)}) copy-start(pred[32]{0:T(512)(128)(4,1)} %get-tuple-element.105) | copy-start | bytes 100
  50.9 9.1 %copy-start.4 = (f32[7]{0:T(128)S(1)}, f32[7]{0:T(128)}, u32[]{:S(2)}) copy-start(f32[7]{0:T(128)} %param.10) | copy-start | bytes 88
  50.9 9.1 %copy-start.5 = (f32[7]{0:T(128)S(1)}, f32[7]{0:T(128)}, u32[]{:S(2)}) copy-start(f32[7]{0:T(128)} %param.11) | copy-start | bytes 88
where the time goes:
time: 122 us; the launch traced here: 121 us
  other arithmetic  33.8 us (28%)
  local copies, waits for them, and re-layouts  28.9 us (24%)
  starting transfers between devices  21.2 us (17%)
  waiting for transfers between devices  18.9 us (15%)
  loops' own time  13.9 us (11%)
  matrix products  3.38 us (3%)
    add x7, other arithmetic, advance_quantity(): jnp.maximum(velocity, 0.0) * left_state  17.4 us
    another operation x1, loops' own time, body(): lax.map(lambda entry: advance_quantity(entry[0], occupied, entry[1], entr...  13.9 us
    all_to_all x1, waiting for transfers between devices, body(): lax.all_to_all(outgoing, 'dev', split_axis=0, concat_axis=0, tiled=True)  12.6 us
    dynamic_slice x14, local copies, waits for them, and re-layouts, body(): lax.map(lambda entry: advance_quantity(entry[0], occupied, entry[1], entr...  8.53 us
    squeeze x7, local copies, waits for them, and re-layouts, body(): lax.map(lambda entry: advance_quantity(entry[0], occupied, entry[1], entr...  8.25 us
    ppermute x2, starting transfers between devices, extended_2(): lax.ppermute(lax.slice_in_dim(block, block.shape[dim] - width, None, axis...  7.62 us
    dynamic_update_slice x7, local copies, waits for them, and re-layouts, body(): lax.map(lambda entry: advance_quantity(entry[0], occupied, entry[1], entr...  6 us
    ppermute x2, starting transfers between devices, extended_2(): lax.ppermute(lax.slice_in_dim(block, 0, width, axis=dim), axis, backward)  5.78 us
  transfers between devices with their start and end apart: 6, of which 4 were waited for; matrix products, arithmetic and copies ran while one was open for 6% of the time, Pallas kernels for 0%

commit v1 on v0

v1 whole, which is shorter than its diff:
```python
import functools

import jax
import jax.numpy as jnp
from jax import lax
from jax.experimental import pallas as pl
from jax.experimental.pallas import tpu as pltpu
from jax.sharding import PartitionSpec as P

NEW_CAP = 32
GHOST = 3
COURANT = 0.4
WENO_EPS = 1e-06
MESH = pl.DeviceIdType.MESH


def iota(shape, dim):
    return lax.broadcasted_iota(jnp.int32, shape, dim)


def split_low(values, size):
    return values & (size - 1)


def split_high(values, size):
    return values >> (size.bit_length() - 1)


def pack_kernel(owners, pair, dest_ref, level_ref, block_ref, out_ref, tags_ref, place_ref):
    slots, _, edge, plane = block_ref.shape
    rows = edge * pair
    lanes = slots * edge

    @pl.when(pl.program_id(0) == 0)
    def _():
        dest = [dest_ref[s] for s in range(slots)]
        within = []
        for s in range(slots):
            count = jnp.int32(0)
            for before in range(s):
                count = count + jnp.where(dest[before] == dest[s], 1, 0)
            within.append(count)
        lane = iota((1, lanes), 1)
        slot_of = split_high(lane, edge)
        target = jnp.zeros((1, lanes), jnp.int32)
        for s in range(slots):
            target = jnp.where(slot_of == s, dest[s] * rows + within[s], target)
        target = target + split_low(lane, edge) * pair
        hit = iota((owners * rows, lanes), 0) == target
        place_ref[...] = jnp.where(hit, 1.0, 0.0).astype(jnp.bfloat16)
        owner = iota(tags_ref.shape, 0)
        slot = split_low(iota(tags_ref.shape, 2), pair)
        tags = jnp.zeros(tags_ref.shape, jnp.int32)
        for s in range(slots):
            here = (owner == dest[s]) & (slot == within[s])
            tags = jnp.where(here, level_ref[s] + 1, tags)
        tags_ref[...] = tags

    payload = block_ref[...].reshape(lanes, plane)
    packed = jnp.dot(place_ref[...], payload, preferred_element_type=jnp.float32)
    out_ref[...] = packed.astype(jnp.bfloat16).reshape(owners, 1, rows, plane)


def advance_tile(cells, neg, speed, threshold):
    total = len(cells)
    edge = total - 2 * GHOST
    m = [jnp.where(neg, cells[total - 1 - i], cells[i]) for i in range(total)]
    d = [m[i + 1] - m[i] for i in range(total - 2)]
    d2 = [x + x for x in d]
    s = [None] + [d[i] - d[i - 1] for i in range(1, total - 2)]
    base = [None] + [(13.0 / 3.0) * (x * x) + 4.0 * WENO_EPS for x in s[1:]]
    shift = []
    for f in range(edge + 1):
        low, high = d[f + 1], d[f + 2]
        t0 = s[f + 1] + d2[f + 1]
        t1 = low + high
        t2 = d2[f + 2] - s[f + 3]
        b0 = base[f + 1] + t0 * t0
        b1 = base[f + 2] + t1 * t1
        b2 = base[f + 3] + t2 * t2
        w0, w1, w2 = b1 * b2, b0 * b2, b0 * b1
        w0, w1, w2 = w0 * w0, 6.0 * (w1 * w1), 3.0 * (w2 * w2)
        p0 = t0 + t0 - low
        p1 = low + d2[f + 2]
        p2 = t2 + high
        shift.append((w0 * p0 + w1 * p1 + w2 * p2) / (w0 + w1 + w2))
    full = COURANT * speed
    sixth = full / 6.0
    moved = [
        m[c + GHOST] - (full * d[c + 2] + sixth * (shift[c + 1] - shift[c]))
        for c in range(edge)
    ]
    adv = [jnp.where(neg, moved[edge - 1 - c], moved[c]) for c in range(edge)]
    result = list(adv)
    for k in range(1, edge, 2):
        guess = 0.5 * (adv[k - 1] + adv[k + 1]) if k + 1 < edge else adv[k - 1]
        detail = adv[k] - guess
        result[k] = guess + detail - jnp.clip(detail, -threshold, threshold)
    return result


def step_kernel(
    owners, groups, pair,
    packed_ref, tags_ref, speed_ref, threshold_ref,
    out_ref, levels_ref,
    inc, tin, unpack, ext, gsend, grecv, own_tag, near_tag, wide, obuf,
    tag_send, tag_recv, self_sem, blk_send, blk_recv,
    near_send, near_recv, gh_send, gh_recv, out_sem,
):
    node = lax.axis_index("node")
    me = lax.axis_index("dev")
    quant = inc.shape[0]
    rows, plane = inc.shape[2], inc.shape[3]
    edge = rows // pair
    cap = own_tag.shape[0]
    has_low = node > 0
    has_high = node < groups - 1

    barrier = pltpu.get_barrier_semaphore()
    for r in range(1, owners):
        pl.semaphore_signal(
            barrier, inc=1, device_id={"dev": lax.rem(me + r, owners)}, device_id_type=MESH
        )

    @pl.when(has_low)
    def _():
        pl.semaphore_signal(barrier, inc=1, device_id={"node": node - 1}, device_id_type=MESH)

    @pl.when(has_high)
    def _():
        pl.semaphore_signal(barrier, inc=1, device_id={"node": node + 1}, device_id_type=MESH)

    nears = (node + groups - 1) // groups + (2 * groups - 2 - node) // groups
    pl.semaphore_wait(barrier, owners - 1 + nears)

    def tag_copy(r):
        return pltpu.make_async_remote_copy(
            src_ref=tags_ref.at[lax.rem(me + r, owners)], dst_ref=tin.at[me],
            send_sem=tag_send.at[r], recv_sem=tag_recv.at[r],
            device_id={"dev": lax.rem(me + r, owners)}, device_id_type=MESH,
        )

    def tag_arrival(r):
        return pltpu.make_async_remote_copy(
            src_ref=tags_ref.at[me], dst_ref=tin.at[lax.rem(me + owners - r, owners)],
            send_sem=tag_send.at[r], recv_sem=tag_recv.at[r],
            device_id={"dev": lax.rem(me + r, owners)}, device_id_type=MESH,
        )

    def block_copy(q, r):
        to = lax.rem(me + r, owners)
        return pltpu.make_async_remote_copy(
            src_ref=packed_ref.at[to, q], dst_ref=inc.at[q, me],
            send_sem=blk_send.at[q, r], recv_sem=blk_recv.at[q, r],
            device_id={"dev": to}, device_id_type=MESH,
        )

    def block_arrival(q, r):
        return pltpu.make_async_remote_copy(
            src_ref=packed_ref.at[me, q], dst_ref=inc.at[q, lax.rem(me + owners - r, owners)],
            send_sem=blk_send.at[q, r], recv_sem=blk_recv.at[q, r],
            device_id={"dev": lax.rem(me + r, owners)}, device_id_type=MESH,
        )

    own_tags = pltpu.make_async_copy(tags_ref.at[me], tin.at[me], tag_send.at[0])

    def own_block(q):
        return pltpu.make_async_copy(packed_ref.at[me, q], inc.at[q, me], self_sem.at[q])

    own_tags.start()
    for r in range(1, owners):
        tag_copy(r).start()

    @pl.loop(0, quant)
    def _(q):
        own_block(q).start()
        for r in range(1, owners):
            block_copy(q, r).start()

    @pl.when(node == 0)
    def _():
        grecv[0] = jnp.zeros(grecv.shape[1:], grecv.dtype)
        near_tag[0] = jnp.zeros(near_tag.shape[1:], near_tag.dtype)

    @pl.when(node == groups - 1)
    def _():
        grecv[1] = jnp.zeros(grecv.shape[1:], grecv.dtype)
        near_tag[1] = jnp.zeros(near_tag.shape[1:], near_tag.dtype)

    own_tags.wait()
    for r in range(1, owners):
        tag_arrival(r).wait_recv()

    lane = iota((1, rows), 1)
    slot, cell = split_low(lane, pair), split_high(lane, pair)
    first = jnp.zeros((1, 1), jnp.float32)
    tag_sum = jnp.zeros((cap, rows), jnp.float32)
    row_p = iota((cap, rows), 0)
    targets = []
    for i in range(owners):
        tag = tin[i, 0:1, :]
        present = tag > 0
        position = first.astype(jnp.int32) + slot
        targets.append(jnp.where(present, cell * cap + position, -1))
        here = (row_p == jnp.where(present & (cell == 0), position, -1))
        tag_sum = tag_sum + jnp.where(here, tag.astype(jnp.float32), 0.0)
        count = jnp.sum(jnp.where(present, 1.0, 0.0), axis=1, keepdims=True)
        first = first + count * (1.0 / edge)
    tag_col = jnp.sum(tag_sum, axis=1, keepdims=True)
    tag_all = jnp.broadcast_to(tag_col, own_tag.shape)
    own_tag[...] = tag_all.astype(jnp.int32)
    levels_ref[...] = jnp.transpose(tag_all)[0:8, :].astype(jnp.int32) - 1
    row = iota((edge * cap, rows), 0)
    for i in range(owners):
        unpack[i] = jnp.where(row == targets[i], 1.0, 0.0).astype(jnp.bfloat16)

    def near_copy(up):
        to = node + 1 if up else node - 1
        index = 0 if up else 1
        return pltpu.make_async_remote_copy(
            src_ref=own_tag, dst_ref=near_tag.at[index],
            send_sem=near_send.at[index], recv_sem=near_recv.at[index],
            device_id={"node": to}, device_id_type=MESH,
        )

    def ghost_copy(q, up):
        to = node + 1 if up else node - 1
        index = 0 if up else 1
        return pltpu.make_async_remote_copy(
            src_ref=gsend.at[index, q], dst_ref=grecv.at[index, q],
            send_sem=gh_send.at[index, q], recv_sem=gh_recv.at[index, q],
            device_id={"node": to}, device_id_type=MESH,
        )

    @pl.when(has_high)
    def _():
        near_copy(True).start()

    @pl.when(has_low)
    def _():
        near_copy(False).start()

    @pl.when(has_low)
    def _():
        near_copy(True).wait_recv()

    @pl.when(has_high)
    def _():
        near_copy(False).wait_recv()

    def front(q):
        at = split_low(q, 2)
        own_block(q).wait()
        for r in range(1, owners):
            block_arrival(q, r).wait_recv()
        total = jnp.dot(unpack[0], inc[q, 0], preferred_element_type=jnp.float32)
        for i in range(1, owners):
            total = total + jnp.dot(unpack[i], inc[q, i], preferred_element_type=jnp.float32)
        ext[at, GHOST : GHOST + edge] = total.reshape(edge, cap, plane)
        for up in (True, False):
            index = 0 if up else 1
            gap = own_tag[...] - near_tag[1 - index]
            for half in range(plane // 128):
                lanes = slice(half * 128, half * 128 + 128)
                near = [
                    ext[at, GHOST + (edge - 1 - k if up else k), :, lanes]
                    for k in range(2 * GHOST)
                ]
                for k in range(GHOST):
                    finer = 0.5 * (near[2 * k] + near[2 * k + 1])
                    ghost = jnp.where(gap > 0, finer, jnp.where(gap < 0, near[k // 2 if k else 0], near[k]))
                    gsend[index, q, GHOST - 1 - k if up else k, :, lanes] = ghost.astype(jnp.bfloat16)

    def send(q):
        @pl.when(has_high)
        def _():
            ghost_copy(q, True).start()

        @pl.when(has_low)
        def _():
            ghost_copy(q, False).start()

    lane_tiles = plane // 128
    tiles = (cap // 8) * lane_tiles

    def tiles_of(q, start, stop):
        at = split_low(q, 2)
        speed, threshold = speed_ref[q], threshold_ref[q]
        neg = jnp.full((8, 128), speed, jnp.float32) < 0.0
        size = jnp.full((8, 128), jnp.abs(speed), jnp.float32)
        bound = jnp.full((8, 128), threshold, jnp.float32)

        def one(tile, carry):
            top = pl.multiple_of((tile // lane_tiles) * 8, 8)
            lanes = pl.ds(pl.multiple_of((tile % lane_tiles) * 128, 128), 128)
            cells = [ext[at, i, pl.ds(top, 8), lanes] for i in range(edge + 2 * GHOST)]
            result = advance_tile(cells, neg, size, bound)
            occupied = own_tag[pl.ds(top, 8), :] > 0
            for c in range(edge):
                value = jnp.where(occupied, result[c], 0.0)
                wide[tile % lane_tiles, pl.ds(top * edge + c, 8, stride=edge), :] = value
            return carry

        lax.fori_loop(start, stop, one, 0)

    def back_first(q):
        at = split_low(q, 2)

        @pl.when(has_low)
        def _():
            ghost_copy(q, True).wait_recv()

        @pl.when(has_high)
        def _():
            ghost_copy(q, False).wait_recv()

        ext[at, 0:GHOST] = grecv[0, q].astype(jnp.float32)
        ext[at, GHOST + edge :] = grecv[1, q].astype(jnp.float32)
        tiles_of(q, 0, tiles // 2)

    def out_copy(q):
        return pltpu.make_async_copy(obuf.at[q], out_ref.at[:, q], out_sem.at[q])

    def back_second(q):
        tiles_of(q, tiles // 2, tiles)
        for half in range(lane_tiles):
            obuf[q, :, :, half * 128 : half * 128 + 128] = (
                wide[half].astype(jnp.bfloat16).reshape(cap, edge, 128)
            )
        out_copy(q).start()

    front(jnp.int32(0))
    send(jnp.int32(0))

    @pl.loop(1, quant)
    def _(q):
        front(q)
        back_first(q - 1)
        send(q)
        back_second(q - 1)

    last = jnp.int32(quant - 1)
    back_first(last)
    back_second(last)

    for r in range(1, owners):
        tag_copy(r).wait_send()

    @pl.when(has_high)
    def _():
        near_copy(True).wait_send()

    @pl.when(has_low)
    def _():
        near_copy(False).wait_send()

    @pl.loop(0, quant)
    def _(q):
        for r in range(1, owners):
            block_copy(q, r).wait_send()

        @pl.when(has_high)
        def _():
            ghost_copy(q, True).wait_send()

        @pl.when(has_low)
        def _():
            ghost_copy(q, False).wait_send()

        out_copy(q).wait()


def body(blocks, levels, destinations, speeds, thresholds):
    owners, groups = lax.axis_size("dev"), lax.axis_size("node")
    _, _, slots, quant, edge, plane = blocks.shape
    pair = max(1, (2 * slots + owners - 1) // owners)
    rows = edge * pair
    smem = pl.BlockSpec(memory_space=pltpu.SMEM)
    anywhere = pl.BlockSpec(memory_space=pl.ANY)
    packed, tags = pl.pallas_call(
        functools.partial(pack_kernel, owners, pair),
        grid=(quant,),
        in_specs=[smem, smem, pl.BlockSpec((slots, 1, edge, plane), lambda q: (0, q, 0, 0))],
        out_specs=[
            pl.BlockSpec((owners, 1, rows, plane), lambda q: (0, q, 0, 0)),
            pl.BlockSpec((owners, 8, rows), lambda q: (0, 0, 0)),
        ],
        out_shape=[
            jax.ShapeDtypeStruct((owners, quant, rows, plane), jnp.bfloat16),
            jax.ShapeDtypeStruct((owners, 8, rows), jnp.int32),
        ],
        scratch_shapes=[pltpu.VMEM((owners * rows, slots * edge), jnp.bfloat16)],
        name="pack",
    )(destinations[0, 0], levels[0, 0], blocks[0, 0])

    cells = edge + 2 * GHOST
    dma = pltpu.SemaphoreType.DMA
    updated, new_levels = pl.pallas_call(
        functools.partial(step_kernel, owners, groups, pair),
        in_specs=[anywhere, anywhere, smem, smem],
        out_specs=[anywhere, pl.BlockSpec(memory_space=pltpu.VMEM)],
        out_shape=[
            jax.ShapeDtypeStruct((NEW_CAP, quant, edge, plane), jnp.bfloat16),
            jax.ShapeDtypeStruct((8, NEW_CAP), jnp.int32),
        ],
        scratch_shapes=[
            pltpu.VMEM((quant, owners, rows, plane), jnp.bfloat16),
            pltpu.VMEM((owners, 8, rows), jnp.int32),
            pltpu.VMEM((owners, edge * NEW_CAP, rows), jnp.bfloat16),
            pltpu.VMEM((2, cells, NEW_CAP, plane), jnp.float32),
            pltpu.VMEM((2, quant, GHOST, NEW_CAP, plane), jnp.bfloat16),
            pltpu.VMEM((2, quant, GHOST, NEW_CAP, plane), jnp.bfloat16),
            pltpu.VMEM((NEW_CAP, 128), jnp.int32),
            pltpu.VMEM((2, NEW_CAP, 128), jnp.int32),
            pltpu.VMEM((plane // 128, NEW_CAP * edge, 128), jnp.float32),
            pltpu.VMEM((quant, NEW_CAP, edge, plane), jnp.bfloat16),
            dma((owners,)), dma((owners,)), dma((quant,)),
            dma((quant, owners)), dma((quant, owners)),
            dma((2,)), dma((2,)), dma((2, quant)), dma((2, quant)), dma((quant,)),
        ],
        compiler_params=pltpu.CompilerParams(
            collective_id=0, has_side_effects=True, vmem_limit_bytes=48 * 1024 * 1024
        ),
        name="step",
    )(packed, tags, speeds, thresholds)
    return (
        updated.reshape(1, 1, NEW_CAP, quant, edge, plane),
        new_levels[0].reshape(1, 1, NEW_CAP),
    )


def solution(mesh):
    return jax.shard_map(
        body,
        mesh=mesh,
        in_specs=(
            P("node", "dev", None, None, None, None),
            P("node", "dev", None),
            P("node", "dev", None),
            P(),
            P(),
        ),
        out_specs=(P("node", "dev", None, None, None, None), P("node", "dev", None)),
        check_vma=False,
    )
```

time: 122 us -> 48.2 us (0.40)
  Pallas kernels: 0 us -> 41.9 us
  other arithmetic: 33.8 us -> 0 us
  local copies, waits for them, and re-layouts: 28.9 us -> 5.27 us
  starting transfers between devices: 21.2 us -> 0 us
  waiting for transfers between devices: 18.9 us -> 0 us
  loops' own time: 13.9 us -> 0 us
  matrix products: 3.38 us -> 0 us
    pallas_call x0 -> x2, Pallas kernels: none -> 41.9 us  [the longest x1 36 us: body(): pl.pallas_call(functools.partial(step_kernel, owners, groups, pair), in_s...]
    add x8 -> x0, other arithmetic: 18 us -> none  [the longest x7 17.4 us: advance_quantity(): jnp.maximum(velocity, 0.0) * left_state]
    another operation x1 -> x0, loops' own time: 13.9 us -> none  [body(): lax.map(lambda entry: advance_quantity(entry[0], occupied, entry[1], entr...]
    ppermute x4 -> x0, starting transfers between devices: 13.4 us -> none  [the longest x2 7.62 us: extended_2(): lax.ppermute(lax.slice_in_dim(block, block.shape[dim] - width, None, axis...]
    all_to_all x2 -> x0, waiting for transfers between devices: 12.7 us -> none  [the longest x1 12.6 us: body(): lax.all_to_all(outgoing, 'dev', split_axis=0, concat_axis=0, tiled=True)]
    dynamic_slice x14 -> x0, local copies, waits for them, and re-layouts: 8.53 us -> none  [body(): lax.map(lambda entry: advance_quantity(entry[0], occupied, entry[1], entr...]
    squeeze x7 -> x0, local copies, waits for them, and re-layouts: 8.25 us -> none  [body(): lax.map(lambda entry: advance_quantity(entry[0], occupied, entry[1], entr...]
    all_to_all x2 -> x0, starting transfers between devices: 7.84 us -> none  [the longest x1 4.25 us: body(): lax.all_to_all(outgoing_tags, 'dev', split_axis=0, concat_axis=0, tiled=T...]
  transfers between devices with their start and end apart: 6 -> 0, of which waited for: 4 -> 0; matrix products, arithmetic and copies ran while one was open for 6% -> 0% of each run, Pallas kernels for 0% -> 0%
where the time goes in v1:
time: 48.2 us; the launch traced here: 47.9 us
  Pallas kernels  41.9 us (87%)
  local copies, waits for them, and re-layouts  5.27 us (11%)
  between operations  0.64 us (1%)
    pallas_call x1, Pallas kernels, body(): pl.pallas_call(functools.partial(step_kernel, owners, groups, pair), in_s...  36 us
    pallas_call x1, Pallas kernels, body(): pl.pallas_call(functools.partial(pack_kernel, owners, pair), grid=(quant,...  5.9 us
    unnamed x9, local copies, waits for them, and re-layouts  4.75 us

profile of v1, /device:TPU:1, one launch (start us, length us, event | category | flops | bytes accessed | tf_op | source)
XLA Modules:
  0.0 47.9 jit_solution(5184968398473672341)
XLA Ops:
  0.6 5.9 %pack.1 = (bf16[4,7,128,256]{3,2,1,0:T(8,128)(2,1)}, s32[4,8,128]{2,1,0:T(8,128)}) custom-call(s32[16]{0:T(128)} %bitcast.8, s32[16]{0:T(128)} %bitcast.9, bf16[16,7,16,256]{3,2,1,0:T(8,128)(2,1)} %bitcast.7), custom_call_target="tpu_custom_call" | custom-call | tf_op jit(solution)/shard_map/pack/pallas_call | solution.py:380
  6.5 0.0 copy-start
  6.5 1.5 %copy-done = bf16[4,7,128,256]{3,2,1,0:T(8,128)(2,1)S(1)} copy-done((bf16[4,7,128,256]{3,2,1,0:T(8,128)(2,1)S(1)}, bf16[4,7,128,256]{3,2,1,0:T(8,128)(2,1)}, u32[]{:S(2)}) %copy-start) | copy-done | bytes 1835032
  8.0 0.0 copy-start.1
  8.0 0.7 %copy-done.1 = s32[4,8,128]{2,1,0:T(8,128)S(1)} copy-done((s32[4,8,128]{2,1,0:T(8,128)S(1)}, s32[4,8,128]{2,1,0:T(8,128)}, u32[]{:S(2)}) %copy-start.1) | copy-done | bytes 16408
  8.8 0.0 copy-start.2
  8.8 0.7 %copy-done.2 = f32[7]{0:T(128)S(1)} copy-done((f32[7]{0:T(128)S(1)}, f32[7]{0:T(128)}, u32[]{:S(2)}) %copy-start.2) | copy-done | bytes 52
  9.4 0.0 copy-start.3
  9.4 0.7 %copy-done.3 = f32[7]{0:T(128)S(1)} copy-done((f32[7]{0:T(128)S(1)}, f32[7]{0:T(128)}, u32[]{:S(2)}) %copy-start.3) | copy-done | bytes 52
  10.1 36.0 %step.1 = (bf16[32,7,16,256]{3,2,1,0:T(8,128)(2,1)S(1)}, s32[8,32]{1,0:T(8,128)S(1)}) custom-call(bf16[4,7,128,256]{3,2,1,0:T(8,128)(2,1)S(1)} %copy-done, s32[4,8,128]{2,1,0:T(8,128)S(1)} %copy-done.1, f32[7]{0:T(128)S(1)} %copy-done.2, f32[7]{0:T(128)S(1)} %copy-done.3), custom_call_target="tpu_custom_call" | custom-call | tf_op jit(solution)/shard_map/step/pallas_call | solution.py:398
  46.1 0.5 %slice_bitcast_fusion = s32[1,1,32]{2,1,0:T(1,128)} fusion(s32[8,32]{1,0:T(8,128)S(1)} %get-tuple-element.9), kind=kLoop, calls=%fused_computation | loop fusion | bytes 256 | tf_op jit(solution)/shard_map/reshape;squeeze | solution.py:428
  46.6 1.2 %copy.8 = bf16[1,1,32,7,16,256]{5,4,3,2,1,0:T(8,128)(2,1)} copy(bf16[1,1,32,7,16,256]{5,4,3,2,1,0:T(8,128)(2,1)S(1)} %bitcast.6) | data formatting | bytes 3670016
Async XLA Ops:
  6.5 1.5 %copy-start = (bf16[4,7,128,256]{3,2,1,0:T(8,128)(2,1)S(1)}, bf16[4,7,128,256]{3,2,1,0:T(8,128)(2,1)}, u32[]{:S(2)}) copy-start(bf16[4,7,128,256]{3,2,1,0:T(8,128)(2,1)} %get-tuple-element.6.packed_ref) | copy-start | bytes 5505028
  8.0 0.7 %copy-start.1 = (s32[4,8,128]{2,1,0:T(8,128)S(1)}, s32[4,8,128]{2,1,0:T(8,128)}, u32[]{:S(2)}) copy-start(s32[4,8,128]{2,1,0:T(8,128)} %get-tuple-element.7.tags_ref) | copy-start | bytes 49156
  8.8 0.7 %copy-start.2 = (f32[7]{0:T(128)S(1)}, f32[7]{0:T(128)}, u32[]{:S(2)}) copy-start(f32[7]{0:T(128)} %speed_ref.1) | copy-start | bytes 88
  9.4 0.7 %copy-start.3 = (f32[7]{0:T(128)S(1)}, f32[7]{0:T(128)}, u32[]{:S(2)}) copy-start(f32[7]{0:T(128)} %threshold_ref.1) | copy-start | bytes 88

commit v2 on v1

--- a/solution.py
+++ b/solution.py
@@ -26,39 +26,32 @@
     return values >> (size.bit_length() - 1)
 
 
-def pack_kernel(owners, pair, dest_ref, level_ref, block_ref, out_ref, tags_ref, place_ref):
-    slots, _, edge, plane = block_ref.shape
+def plan_sends(owners, pair, edge, dest_ref, level_ref, place_ref, tags_ref):
+    slots = dest_ref.shape[0]
     rows = edge * pair
     lanes = slots * edge
-
-    @pl.when(pl.program_id(0) == 0)
-    def _():
-        dest = [dest_ref[s] for s in range(slots)]
-        within = []
-        for s in range(slots):
-            count = jnp.int32(0)
-            for before in range(s):
-                count = count + jnp.where(dest[before] == dest[s], 1, 0)
-            within.append(count)
-        lane = iota((1, lanes), 1)
-        slot_of = split_high(lane, edge)
-        target = jnp.zeros((1, lanes), jnp.int32)
-        for s in range(slots):
-            target = jnp.where(slot_of == s, dest[s] * rows + within[s], target)
-        target = target + split_low(lane, edge) * pair
-        hit = iota((owners * rows, lanes), 0) == target
-        place_ref[...] = jnp.where(hit, 1.0, 0.0).astype(jnp.bfloat16)
-        owner = iota(tags_ref.shape, 0)
-        slot = split_low(iota(tags_ref.shape, 2), pair)
-        tags = jnp.zeros(tags_ref.shape, jnp.int32)
-        for s in range(slots):
-            here = (owner == dest[s]) & (slot == within[s])
-            tags = jnp.where(here, level_ref[s] + 1, tags)
-        tags_ref[...] = tags
-
-    payload = block_ref[...].reshape(lanes, plane)
-    packed = jnp.dot(place_ref[...], payload, preferred_element_type=jnp.float32)
-    out_ref[...] = packed.astype(jnp.bfloat16).reshape(owners, 1, rows, plane)
+    dest = [dest_ref[s] for s in range(slots)]
+    within = []
+    for s in range(slots):
+        count = jnp.int32(0)
+        for before in range(s):
+            count = count + jnp.where(dest[before] == dest[s], 1, 0)
+        within.append(count)
+    lane = iota((1, lanes), 1)
+    slot_of = split_high(lane, edge)
+    target = jnp.zeros((1, lanes), jnp.int32)
+    for s in range(slots):
+        target = jnp.where(slot_of == s, dest[s] * rows + within[s], target)
+    target = target + split_low(lane, edge) * pair
+    hit = iota((owners * rows, lanes), 0) == target
+    place_ref[...] = jnp.where(hit, 1.0, 0.0).astype(jnp.bfloat16)
+    owner = iota(tags_ref.shape, 0)
+    slot = split_low(iota(tags_ref.shape, 2), pair)
+    tags = jnp.zeros(tags_ref.shape, jnp.int32)
+    for s in range(slots):
+        here = (owner == dest[s]) & (slot == within[s])
+        tags = jnp.where(here, level_ref[s] + 1, tags)
+    tags_ref[...] = tags
 
 
 def advance_tile(cells, neg, speed, threshold):
@@ -101,20 +94,40 @@
 
 def step_kernel(
     owners, groups, pair,
-    packed_ref, tags_ref, speed_ref, threshold_ref,
+    dest_hbm, level_hbm, block_hbm, speed_hbm, threshold_hbm,
     out_ref, levels_ref,
+    dest_ref, level_ref, speed_ref, threshold_ref,
+    payload, place, packed_ref, tags_ref,
     inc, tin, unpack, ext, gsend, grecv, own_tag, near_tag, wide, obuf,
-    tag_send, tag_recv, self_sem, blk_send, blk_recv,
+    load_sem, block_sem, tag_send, tag_recv, blk_send, blk_recv,
     near_send, near_recv, gh_send, gh_recv, out_sem,
 ):
     node = lax.axis_index("node")
     me = lax.axis_index("dev")
-    quant = inc.shape[0]
-    rows, plane = inc.shape[2], inc.shape[3]
-    edge = rows // pair
+    slots, quant, edge, plane = block_hbm.shape
+    rows = edge * pair
     cap = own_tag.shape[0]
     has_low = node > 0
     has_high = node < groups - 1
+
+    small = [
+        pltpu.make_async_copy(source, target, load_sem.at[n])
+        for n, (source, target) in enumerate(
+            (
+                (dest_hbm, dest_ref), (level_hbm, level_ref),
+                (speed_hbm, speed_ref), (threshold_hbm, threshold_ref),
+            )
+        )
+    ]
+    for copy in small:
+        copy.start()
+
+    def load(q):
+        return pltpu.make_async_copy(block_hbm.at[:, q], payload.at[q], block_sem.at[q])
+
+    @pl.loop(0, quant)
+    def _(q):
+        load(q).start()
 
     barrier = pltpu.get_barrier_semaphore()
     for r in range(1, owners):
@@ -130,6 +143,9 @@
     def _():
         pl.semaphore_signal(barrier, inc=1, device_id={"node": node + 1}, device_id_type=MESH)
 
+    for copy in small:
+        copy.wait()
+    plan_sends(owners, pair, edge, dest_ref, level_ref, place, tags_ref)
     nears = (node + groups - 1) // groups + (2 * groups - 2 - node) // groups
     pl.semaphore_wait(barrier, owners - 1 + nears)
 
@@ -150,32 +166,41 @@
     def block_copy(q, r):
         to = lax.rem(me + r, owners)
         return pltpu.make_async_remote_copy(
-            src_ref=packed_ref.at[to, q], dst_ref=inc.at[q, me],
+            src_ref=packed_ref.at[q, to], dst_ref=inc.at[q, me],
             send_sem=blk_send.at[q, r], recv_sem=blk_recv.at[q, r],
             device_id={"dev": to}, device_id_type=MESH,
         )
 
     def block_arrival(q, r):
         return pltpu.make_async_remote_copy(
-            src_ref=packed_ref.at[me, q], dst_ref=inc.at[q, lax.rem(me + owners - r, owners)],
+            src_ref=packed_ref.at[q, me], dst_ref=inc.at[q, lax.rem(me + owners - r, owners)],
             send_sem=blk_send.at[q, r], recv_sem=blk_recv.at[q, r],
             device_id={"dev": lax.rem(me + r, owners)}, device_id_type=MESH,
         )
 
-    own_tags = pltpu.make_async_copy(tags_ref.at[me], tin.at[me], tag_send.at[0])
-
-    def own_block(q):
-        return pltpu.make_async_copy(packed_ref.at[me, q], inc.at[q, me], self_sem.at[q])
-
-    own_tags.start()
+    def pack(q):
+        load(q).wait()
+        flat = payload[q].reshape(slots * edge, plane)
+        rows_of = jnp.dot(place[...], flat, preferred_element_type=jnp.float32)
+        packed_ref[q] = rows_of.astype(jnp.bfloat16).reshape(owners, rows, plane)
+
+    def launch(q):
+        for r in range(1, owners):
+            block_copy(q, r).start()
+
+    tin[me] = tags_ref[me]
+    pack(jnp.int32(0))
     for r in range(1, owners):
         tag_copy(r).start()
 
-    @pl.loop(0, quant)
+    @pl.loop(1, quant)
     def _(q):
-        own_block(q).start()
-        for r in range(1, owners):
-            block_copy(q, r).start()
+        pack(q)
+        launch(q - 1)
+        inc[q - 1, me] = packed_ref[q - 1, me]
+
+    launch(jnp.int32(quant - 1))
+    inc[quant - 1, me] = packed_ref[quant - 1, me]
 
     @pl.when(node == 0)
     def _():
@@ -187,7 +212,6 @@
         grecv[1] = jnp.zeros(grecv.shape[1:], grecv.dtype)
         near_tag[1] = jnp.zeros(near_tag.shape[1:], near_tag.dtype)
 
-    own_tags.wait()
     for r in range(1, owners):
         tag_arrival(r).wait_recv()
 
@@ -212,7 +236,8 @@
     levels_ref[...] = jnp.transpose(tag_all)[0:8, :].astype(jnp.int32) - 1
     row = iota((edge * cap, rows), 0)
     for i in range(owners):
-        unpack[i] = jnp.where(row == targets[i], 1.0, 0.0).astype(jnp.bfloat16)
+        hit = jnp.where(row == targets[i], 1.0, 0.0).astype(jnp.bfloat16)
+        unpack[:, i * rows : i * rows + rows] = hit
 
     def near_copy(up):
         to = node + 1 if up else node - 1
@@ -250,12 +275,11 @@
 
     def front(q):
         at = split_low(q, 2)
-        own_block(q).wait()
         for r in range(1, owners):
             block_arrival(q, r).wait_recv()
-        total = jnp.dot(unpack[0], inc[q, 0], preferred_element_type=jnp.float32)
-        for i in range(1, owners):
-            total = total + jnp.dot(unpack[i], inc[q, i], preferred_element_type=jnp.float32)
+        total = jnp.dot(
+            unpack[...], inc[q].reshape(owners * rows, plane), preferred_element_type=jnp.float32
+        )
         ext[at, GHOST : GHOST + edge] = total.reshape(edge, cap, plane)
         for up in (True, False):
             index = 0 if up else 1
@@ -375,38 +399,28 @@
     _, _, slots, quant, edge, plane = blocks.shape
     pair = max(1, (2 * slots + owners - 1) // owners)
     rows = edge * pair
-    smem = pl.BlockSpec(memory_space=pltpu.SMEM)
-    anywhere = pl.BlockSpec(memory_space=pl.ANY)
-    packed, tags = pl.pallas_call(
-        functools.partial(pack_kernel, owners, pair),
-        grid=(quant,),
-        in_specs=[smem, smem, pl.BlockSpec((slots, 1, edge, plane), lambda q: (0, q, 0, 0))],
-        out_specs=[
-            pl.BlockSpec((owners, 1, rows, plane), lambda q: (0, q, 0, 0)),
-            pl.BlockSpec((owners, 8, rows), lambda q: (0, 0, 0)),
-        ],
-        out_shape=[
-            jax.ShapeDtypeStruct((owners, quant, rows, plane), jnp.bfloat16),
-            jax.ShapeDtypeStruct((owners, 8, rows), jnp.int32),
-        ],
-        scratch_shapes=[pltpu.VMEM((owners * rows, slots * edge), jnp.bfloat16)],
-        name="pack",
-    )(destinations[0, 0], levels[0, 0], blocks[0, 0])
-
     cells = edge + 2 * GHOST
     dma = pltpu.SemaphoreType.DMA
     updated, new_levels = pl.pallas_call(
         functools.partial(step_kernel, owners, groups, pair),
-        in_specs=[anywhere, anywhere, smem, smem],
-        out_specs=[anywhere, pl.BlockSpec(memory_space=pltpu.VMEM)],
+        in_specs=[pl.BlockSpec(memory_space=pltpu.HBM)] * 5,
+        out_specs=[
+            pl.BlockSpec(memory_space=pltpu.HBM), pl.BlockSpec(memory_space=pltpu.VMEM)
+        ],
         out_shape=[
             jax.ShapeDtypeStruct((NEW_CAP, quant, edge, plane), jnp.bfloat16),
             jax.ShapeDtypeStruct((8, NEW_CAP), jnp.int32),
         ],
         scratch_shapes=[
+            pltpu.SMEM((slots,), jnp.int32), pltpu.SMEM((slots,), jnp.int32),
+            pltpu.SMEM((quant,), jnp.float32), pltpu.SMEM((quant,), jnp.float32),
+            pltpu.VMEM((quant, slots, edge, plane), jnp.bfloat16),
+            pltpu.VMEM((owners * rows, slots * edge), jnp.bfloat16),
             pltpu.VMEM((quant, owners, rows, plane), jnp.bfloat16),
             pltpu.VMEM((owners, 8, rows), jnp.int32),
-            pltpu.VMEM((owners, edge * NEW_CAP, rows), jnp.bfloat16),
+            pltpu.VMEM((quant, owners, rows, plane), jnp.bfloat16),
+            pltpu.VMEM((owners, 8, rows), jnp.int32),
+            pltpu.VMEM((edge * NEW_CAP, owners * rows), jnp.bfloat16),
             pltpu.VMEM((2, cells, NEW_CAP, plane), jnp.float32),
             pltpu.VMEM((2, quant, GHOST, NEW_CAP, plane), jnp.bfloat16),
             pltpu.VMEM((2, quant, GHOST, NEW_CAP, plane), jnp.bfloat16),
@@ -414,15 +428,15 @@
             pltpu.VMEM((2, NEW_CAP, 128), jnp.int32),
             pltpu.VMEM((plane // 128, NEW_CAP * edge, 128), jnp.float32),
             pltpu.VMEM((quant, NEW_CAP, edge, plane), jnp.bfloat16),
-            dma((owners,)), dma((owners,)), dma((quant,)),
+            dma((4,)), dma((quant,)), dma((owners,)), dma((owners,)),
             dma((quant, owners)), dma((quant, owners)),
             dma((2,)), dma((2,)), dma((2, quant)), dma((2, quant)), dma((quant,)),
         ],
         compiler_params=pltpu.CompilerParams(
-            collective_id=0, has_side_effects=True, vmem_limit_bytes=48 * 1024 * 1024
+            collective_id=0, has_side_effects=True, vmem_limit_bytes=67_000_000
         ),
         name="step",
-    )(packed, tags, speeds, thresholds)
+    )(destinations[0, 0], levels[0, 0], blocks[0, 0], speeds, thresholds)
     return (
         updated.reshape(1, 1, NEW_CAP, quant, edge, plane),
         new_levels[0].reshape(1, 1, NEW_CAP),

time: 48.2 us -> 41 us (0.85)
  Pallas kernels: 41.9 us -> 36.1 us
  local copies, waits for them, and re-layouts: 5.27 us -> 4.03 us
    pallas_call x1 -> x0, Pallas kernels: 5.9 us -> none  [body(): pl.pallas_call(functools.partial(pack_kernel, owners, pair), grid=(quant,...]
    unnamed x9 -> x1, local copies, waits for them, and re-layouts: 4.75 us -> 2.85 us
    another operation x1, local copies, waits for them, and re-layouts: 0.51 us -> 1.18 us  [body(): new_levels[0].reshape(1, 1, NEW_CAP)]
where the time goes in v2:
time: 41 us; the launch traced here: 40.8 us
  Pallas kernels  36.1 us (88%)
  local copies, waits for them, and re-layouts  4.03 us (10%)
  between operations  0.64 us (2%)
    pallas_call x1, Pallas kernels, body(): pl.pallas_call(functools.partial(step_kernel, owners, groups, pair), in_s...  36.1 us
    unnamed x1, local copies, waits for them, and re-layouts  2.85 us
    another operation x1, local copies, waits for them, and re-layouts, body(): new_levels[0].reshape(1, 1, NEW_CAP)  1.18 us

profile of v2, /device:TPU:1, one launch (start us, length us, event | category | flops | bytes accessed | tf_op | source)
XLA Modules:
  0.0 40.8 jit_solution(11335295494557287870)
XLA Ops:
  0.6 36.1 %step.1 = (bf16[32,7,16,256]{3,2,1,0:T(8,128)(2,1)}, s32[8,32]{1,0:T(8,128)}) custom-call(s32[16]{0:T(128)} %bitcast.8, s32[16]{0:T(128)} %bitcast.9, bf16[16,7,16,256]{3,2,1,0:T(8,128)(2,1)} %bitcast.7, f32[7]{0:T(128)} %speed_hbm.1, f32[7]{0:T(128)} %threshold_hbm.1), custom_call_target="tpu_custom_call" | custom-call | tf_op jit(solution)/shard_map/step/pallas_call | solution.py:404
  36.8 1.2 %slice_bitcast_fusion = s32[1,1,32]{2,1,0:T(1,128)} fusion(s32[8,32]{1,0:T(8,128)} %get-tuple-element.5), kind=kLoop, calls=%fused_computation | loop fusion | bytes 256 | tf_op jit(solution)/shard_map/reshape;squeeze | solution.py:442
  38.0 2.9 %copy.8 = bf16[1,1,32,7,16,256]{5,4,3,2,1,0:T(8,128)(2,1)} copy(bf16[1,1,32,7,16,256]{5,4,3,2,1,0:T(8,128)(2,1)} %bitcast.6) | data formatting | bytes 3670016

commit v3 on v2

--- a/solution.py
+++ b/solution.py
@@ -20,6 +20,15 @@
 
 def split_low(values, size):
     return values & (size - 1)
+
+
+def partner(me, r):
+    result, bit = 0, 1
+    while bit <= r:
+        own = me // bit % 2
+        result = result + bit * ((1 - own) if r & bit else own)
+        bit *= 2
+    return result + me // bit * bit
 
 
 def split_high(values, size):
@@ -132,7 +141,7 @@
     barrier = pltpu.get_barrier_semaphore()
     for r in range(1, owners):
         pl.semaphore_signal(
-            barrier, inc=1, device_id={"dev": lax.rem(me + r, owners)}, device_id_type=MESH
+            barrier, inc=1, device_id={"dev": partner(me, r)}, device_id_type=MESH
         )
 
     @pl.when(has_low)
@@ -151,20 +160,20 @@
 
     def tag_copy(r):
         return pltpu.make_async_remote_copy(
-            src_ref=tags_ref.at[lax.rem(me + r, owners)], dst_ref=tin.at[me],
+            src_ref=tags_ref.at[partner(me, r)], dst_ref=tin.at[me],
             send_sem=tag_send.at[r], recv_sem=tag_recv.at[r],
-            device_id={"dev": lax.rem(me + r, owners)}, device_id_type=MESH,
+            device_id={"dev": partner(me, r)}, device_id_type=MESH,
         )
 
     def tag_arrival(r):
         return pltpu.make_async_remote_copy(
-            src_ref=tags_ref.at[me], dst_ref=tin.at[lax.rem(me + owners - r, owners)],
+            src_ref=tags_ref.at[me], dst_ref=tin.at[partner(me, r)],
             send_sem=tag_send.at[r], recv_sem=tag_recv.at[r],
-            device_id={"dev": lax.rem(me + r, owners)}, device_id_type=MESH,
+            device_id={"dev": partner(me, r)}, device_id_type=MESH,
         )
 
     def block_copy(q, r):
-        to = lax.rem(me + r, owners)
+        to = partner(me, r)
         return pltpu.make_async_remote_copy(
             src_ref=packed_ref.at[q, to], dst_ref=inc.at[q, me],
             send_sem=blk_send.at[q, r], recv_sem=blk_recv.at[q, r],
@@ -173,9 +182,9 @@
 
     def block_arrival(q, r):
         return pltpu.make_async_remote_copy(
-            src_ref=packed_ref.at[q, me], dst_ref=inc.at[q, lax.rem(me + owners - r, owners)],
+            src_ref=packed_ref.at[q, me], dst_ref=inc.at[q, partner(me, r)],
             send_sem=blk_send.at[q, r], recv_sem=blk_recv.at[q, r],
-            device_id={"dev": lax.rem(me + r, owners)}, device_id_type=MESH,
+            device_id={"dev": partner(me, r)}, device_id_type=MESH,
         )
 
     def pack(q):
@@ -277,10 +286,16 @@
         at = split_low(q, 2)
         for r in range(1, owners):
             block_arrival(q, r).wait_recv()
-        total = jnp.dot(
-            unpack[...], inc[q].reshape(owners * rows, plane), preferred_element_type=jnp.float32
-        )
-        ext[at, GHOST : GHOST + edge] = total.reshape(edge, cap, plane)
+        sources = inc[q].reshape(owners * rows, plane)
+
+        def arrange(low, high):
+            part = jnp.dot(
+                unpack[low * cap : high * cap, :], sources, preferred_element_type=jnp.float32
+            )
+            ext[at, GHOST + low : GHOST + high] = part.reshape(high - low, cap, plane)
+
+        arrange(0, 2 * GHOST)
+        arrange(edge - 2 * GHOST, edge)
         for up in (True, False):
             index = 0 if up else 1
             gap = own_tag[...] - near_tag[1 - index]
@@ -294,6 +309,7 @@
                     finer = 0.5 * (near[2 * k] + near[2 * k + 1])
                     ghost = jnp.where(gap > 0, finer, jnp.where(gap < 0, near[k // 2 if k else 0], near[k]))
                     gsend[index, q, GHOST - 1 - k if up else k, :, lanes] = ghost.astype(jnp.bfloat16)
+        arrange(2 * GHOST, edge - 2 * GHOST)
 
     def send(q):
         @pl.when(has_high)
@@ -307,7 +323,7 @@
     lane_tiles = plane // 128
     tiles = (cap // 8) * lane_tiles
 
-    def tiles_of(q, start, stop):
+    def tiles_of(q):
         at = split_low(q, 2)
         speed, threshold = speed_ref[q], threshold_ref[q]
         neg = jnp.full((8, 128), speed, jnp.float32) < 0.0
@@ -325,9 +341,12 @@
                 wide[tile % lane_tiles, pl.ds(top * edge + c, 8, stride=edge), :] = value
             return carry
 
-        lax.fori_loop(start, stop, one, 0)
-
-    def back_first(q):
+        lax.fori_loop(0, tiles, one, 0)
+
+    def out_copy(q):
+        return pltpu.make_async_copy(obuf.at[q], out_ref.at[:, q], out_sem.at[q])
+
+    def back(q):
         at = split_low(q, 2)
 
         @pl.when(has_low)
@@ -340,13 +359,7 @@
 
         ext[at, 0:GHOST] = grecv[0, q].astype(jnp.float32)
         ext[at, GHOST + edge :] = grecv[1, q].astype(jnp.float32)
-        tiles_of(q, 0, tiles // 2)
-
-    def out_copy(q):
-        return pltpu.make_async_copy(obuf.at[q], out_ref.at[:, q], out_sem.at[q])
-
-    def back_second(q):
-        tiles_of(q, tiles // 2, tiles)
+        tiles_of(q)
         for half in range(lane_tiles):
             obuf[q, :, :, half * 128 : half * 128 + 128] = (
                 wide[half].astype(jnp.bfloat16).reshape(cap, edge, 128)
@@ -359,13 +372,11 @@
     @pl.loop(1, quant)
     def _(q):
         front(q)
-        back_first(q - 1)
         send(q)
-        back_second(q - 1)
+        back(q - 1)
 
     last = jnp.int32(quant - 1)
-    back_first(last)
-    back_second(last)
+    back(last)
 
     for r in range(1, owners):
         tag_copy(r).wait_send()

time: 41 us -> 38.3 us (0.934)
  Pallas kernels: 36.1 us -> 33.5 us
    pallas_call x1, Pallas kernels: 36.1 us -> 33.5 us  [body(): pl.pallas_call(functools.partial(step_kernel, owners, groups, pair), in_s...]
where the time goes in v3:
time: 38.3 us; the launch traced here: 38.1 us
  Pallas kernels  33.5 us (87%)
  local copies, waits for them, and re-layouts  4.03 us (11%)
  between operations  0.64 us (2%)
    pallas_call x1, Pallas kernels, body(): pl.pallas_call(functools.partial(step_kernel, owners, groups, pair), in_s...  33.5 us
    unnamed x1, local copies, waits for them, and re-layouts  2.85 us
    another operation x1, local copies, waits for them, and re-layouts, body(): new_levels[0].reshape(1, 1, NEW_CAP)  1.18 us

profile of v3, /device:TPU:1, one launch (start us, length us, event | category | flops | bytes accessed | tf_op | source)
XLA Modules:
  0.0 38.1 jit_solution(2955108212991376048)
XLA Ops:
  0.6 33.5 %step.1 = (bf16[32,7,16,256]{3,2,1,0:T(8,128)(2,1)}, s32[8,32]{1,0:T(8,128)}) custom-call(s32[16]{0:T(128)} %bitcast.8, s32[16]{0:T(128)} %bitcast.9, bf16[16,7,16,256]{3,2,1,0:T(8,128)(2,1)} %bitcast.7, f32[7]{0:T(128)} %speed_hbm.1, f32[7]{0:T(128)} %threshold_hbm.1), custom_call_target="tpu_custom_call" | custom-call | tf_op jit(solution)/shard_map/step/pallas_call | solution.py:415
  34.1 1.2 %slice_bitcast_fusion = s32[1,1,32]{2,1,0:T(1,128)} fusion(s32[8,32]{1,0:T(8,128)} %get-tuple-element.5), kind=kLoop, calls=%fused_computation | loop fusion | bytes 256 | tf_op jit(solution)/shard_map/reshape;squeeze | solution.py:453
  35.3 2.9 %copy.8 = bf16[1,1,32,7,16,256]{5,4,3,2,1,0:T(8,128)(2,1)} copy(bf16[1,1,32,7,16,256]{5,4,3,2,1,0:T(8,128)(2,1)} %bitcast.6) | data formatting | bytes 3670016

commit v4 on v3

--- a/solution.py
+++ b/solution.py
@@ -107,9 +107,9 @@
     out_ref, levels_ref,
     dest_ref, level_ref, speed_ref, threshold_ref,
     payload, place, packed_ref, tags_ref,
-    inc, tin, unpack, ext, gsend, grecv, own_tag, near_tag, wide, obuf,
+    inc, tin, unpack, ext, gsend, grecv, own_tag, near_tag, wide,
     load_sem, block_sem, tag_send, tag_recv, blk_send, blk_recv,
-    near_send, near_recv, gh_send, gh_recv, out_sem,
+    near_send, near_recv, gh_send, gh_recv,
 ):
     node = lax.axis_index("node")
     me = lax.axis_index("dev")
@@ -343,9 +343,6 @@
 
         lax.fori_loop(0, tiles, one, 0)
 
-    def out_copy(q):
-        return pltpu.make_async_copy(obuf.at[q], out_ref.at[:, q], out_sem.at[q])
-
     def back(q):
         at = split_low(q, 2)
 
@@ -361,10 +358,9 @@
         ext[at, GHOST + edge :] = grecv[1, q].astype(jnp.float32)
         tiles_of(q)
         for half in range(lane_tiles):
-            obuf[q, :, :, half * 128 : half * 128 + 128] = (
+            out_ref[:, q, :, half * 128 : half * 128 + 128] = (
                 wide[half].astype(jnp.bfloat16).reshape(cap, edge, 128)
             )
-        out_copy(q).start()
 
     front(jnp.int32(0))
     send(jnp.int32(0))
@@ -401,8 +397,6 @@
         @pl.when(has_low)
         def _():
             ghost_copy(q, False).wait_send()
-
-        out_copy(q).wait()
 
 
 def body(blocks, levels, destinations, speeds, thresholds):
@@ -415,9 +409,7 @@
     updated, new_levels = pl.pallas_call(
         functools.partial(step_kernel, owners, groups, pair),
         in_specs=[pl.BlockSpec(memory_space=pltpu.HBM)] * 5,
-        out_specs=[
-            pl.BlockSpec(memory_space=pltpu.HBM), pl.BlockSpec(memory_space=pltpu.VMEM)
-        ],
+        out_specs=[pl.BlockSpec(memory_space=pltpu.VMEM)] * 2,
         out_shape=[
             jax.ShapeDtypeStruct((NEW_CAP, quant, edge, plane), jnp.bfloat16),
             jax.ShapeDtypeStruct((8, NEW_CAP), jnp.int32),
@@ -438,16 +430,20 @@
             pltpu.VMEM((NEW_CAP, 128), jnp.int32),
             pltpu.VMEM((2, NEW_CAP, 128), jnp.int32),
             pltpu.VMEM((plane // 128, NEW_CAP * edge, 128), jnp.float32),
-            pltpu.VMEM((quant, NEW_CAP, edge, plane), jnp.bfloat16),
             dma((4,)), dma((quant,)), dma((owners,)), dma((owners,)),
             dma((quant, owners)), dma((quant, owners)),
-            dma((2,)), dma((2,)), dma((2, quant)), dma((2, quant)), dma((quant,)),
+            dma((2,)), dma((2,)), dma((2, quant)), dma((2, quant)),
         ],
         compiler_params=pltpu.CompilerParams(
-            collective_id=0, has_side_effects=True, vmem_limit_bytes=67_000_000
+            collective_id=0, has_side_effects=True, vmem_limit_bytes=48 * 1024 * 1024
         ),
         name="step",
-    )(destinations[0, 0], levels[0, 0], blocks[0, 0], speeds, thresholds)
+    )(
+        *(
+            pltpu.with_memory_space_constraint(x, pltpu.HBM)
+            for x in (destinations[0, 0], levels[0, 0], blocks[0, 0], speeds, thresholds)
+        )
+    )
     return (
         updated.reshape(1, 1, NEW_CAP, quant, edge, plane),
         new_levels[0].reshape(1, 1, NEW_CAP),

time: 38.3 us -> 34.7 us (0.906)
  local copies, waits for them, and re-layouts: 4.03 us -> 1.74 us
  Pallas kernels: 33.5 us -> 32.2 us
    unnamed x1, local copies, waits for them, and re-layouts: 2.85 us -> 1.23 us
    pallas_call x1, Pallas kernels: 33.5 us -> 32.2 us  [body(): pl.pallas_call(functools.partial(step_kernel, owners, groups, pair), in_s...]
    another operation x1, local copies, waits for them, and re-layouts: 1.18 us -> 0.51 us  [body(): new_levels[0].reshape(1, 1, NEW_CAP)]
where the time goes in v4:
time: 34.7 us; the launch traced here: 34.6 us
  Pallas kernels  32.2 us (93%)
  local copies, waits for them, and re-layouts  1.74 us (5%)
  between operations  0.64 us (2%)
    pallas_call x1, Pallas kernels, body(): pl.pallas_call(functools.partial(step_kernel, owners, groups, pair), in_s...  32.2 us
    unnamed x1, local copies, waits for them, and re-layouts  1.23 us

profile of v4, /device:TPU:1, one launch (start us, length us, event | category | flops | bytes accessed | tf_op | source)
XLA Modules:
  0.0 34.6 jit_solution(4475068356261978750)
XLA Ops:
  0.6 32.2 %step.1 = (bf16[32,7,16,256]{3,2,1,0:T(8,128)(2,1)S(1)}, s32[8,32]{1,0:T(8,128)S(1)}) custom-call(s32[16]{0:T(128)} %bitcast.8, s32[16]{0:T(128)} %bitcast.9, bf16[16,7,16,256]{3,2,1,0:T(8,128)(2,1)} %bitcast.7, f32[7]{0:T(128)} %speed_hbm.1, f32[7]{0:T(128)} %threshold_hbm.1), custom_call_target="tpu_custom_call" | custom-call | tf_op jit(solution)/shard_map/step/pallas_call | solution.py:409
  32.8 0.5 %slice_bitcast_fusion = s32[1,1,32]{2,1,0:T(1,128)} fusion(s32[8,32]{1,0:T(8,128)S(1)} %get-tuple-element.5), kind=kLoop, calls=%fused_computation | loop fusion | bytes 256 | tf_op jit(solution)/shard_map/reshape;squeeze | solution.py:449
  33.3 1.2 %copy.8 = bf16[1,1,32,7,16,256]{5,4,3,2,1,0:T(8,128)(2,1)} copy(bf16[1,1,32,7,16,256]{5,4,3,2,1,0:T(8,128)(2,1)S(1)} %bitcast.6) | data formatting | bytes 3670016

commit v5 on v4

--- a/solution.py
+++ b/solution.py
@@ -155,9 +155,6 @@
     for copy in small:
         copy.wait()
     plan_sends(owners, pair, edge, dest_ref, level_ref, place, tags_ref)
-    nears = (node + groups - 1) // groups + (2 * groups - 2 - node) // groups
-    pl.semaphore_wait(barrier, owners - 1 + nears)
-
     def tag_copy(r):
         return pltpu.make_async_remote_copy(
             src_ref=tags_ref.at[partner(me, r)], dst_ref=tin.at[me],
@@ -197,19 +194,27 @@
         for r in range(1, owners):
             block_copy(q, r).start()
 
-    tin[me] = tags_ref[me]
+    def keep(q):
+        inc[q, me] = packed_ref[q, me]
+
     pack(jnp.int32(0))
+    nears = (node + groups - 1) // groups + (2 * groups - 2 - node) // groups
+    pl.semaphore_wait(barrier, owners - 1 + nears)
     for r in range(1, owners):
         tag_copy(r).start()
-
-    @pl.loop(1, quant)
+    launch(jnp.int32(0))
+    tin[me] = tags_ref[me]
+    keep(0)
+    pack(jnp.int32(1))
+
+    @pl.loop(2, quant)
     def _(q):
         pack(q)
         launch(q - 1)
-        inc[q - 1, me] = packed_ref[q - 1, me]
+        keep(q - 1)
 
     launch(jnp.int32(quant - 1))
-    inc[quant - 1, me] = packed_ref[quant - 1, me]
+    keep(quant - 1)
 
     @pl.when(node == 0)
     def _():

time: 34.7 us -> 34.7 us (level)
  no operation moved by 1% of the time
where the time goes in v5:
time: 34.7 us; the launch traced here: 34.5 us
  Pallas kernels  32.2 us (93%)
  local copies, waits for them, and re-layouts  1.74 us (5%)
  between operations  0.64 us (2%)
    pallas_call x1, Pallas kernels, body(): pl.pallas_call(functools.partial(step_kernel, owners, groups, pair), in_s...  32.2 us
    unnamed x1, local copies, waits for them, and re-layouts  1.23 us

profile of v5, /device:TPU:1, one launch (start us, length us, event | category | flops | bytes accessed | tf_op | source)
XLA Modules:
  0.0 34.5 jit_solution(6770130636805981592)
XLA Ops:
  0.6 32.2 %step.1 = (bf16[32,7,16,256]{3,2,1,0:T(8,128)(2,1)S(1)}, s32[8,32]{1,0:T(8,128)S(1)}) custom-call(s32[16]{0:T(128)} %bitcast.8, s32[16]{0:T(128)} %bitcast.9, bf16[16,7,16,256]{3,2,1,0:T(8,128)(2,1)} %bitcast.7, f32[7]{0:T(128)} %speed_hbm.1, f32[7]{0:T(128)} %threshold_hbm.1), custom_call_target="tpu_custom_call" | custom-call | tf_op jit(solution)/shard_map/step/pallas_call | solution.py:414
  32.8 0.5 %slice_bitcast_fusion = s32[1,1,32]{2,1,0:T(1,128)} fusion(s32[8,32]{1,0:T(8,128)S(1)} %get-tuple-element.5), kind=kLoop, calls=%fused_computation | loop fusion | bytes 256 | tf_op jit(solution)/shard_map/reshape;squeeze | solution.py:454
  33.3 1.2 %copy.8 = bf16[1,1,32,7,16,256]{5,4,3,2,1,0:T(8,128)(2,1)} copy(bf16[1,1,32,7,16,256]{5,4,3,2,1,0:T(8,128)(2,1)S(1)} %bitcast.6) | data formatting | bytes 3670016
